TPU v7x, 32 devices: a whole 2x2x4 slice. The times are simulated.
32 devices in a mesh: grp: 2 (over y), tile: 4 (over x, core), tp: 4 (over z).
Axes of the slice: x: 2, y: 2, z: 4, core: 2. Of those that a mesh axis runs over, the one named last changes fastest.
Arguments:
- atmos_state: bfloat16 [4096, 1536], P(('grp', 'tile')), may hold values from -6 to 6
- atmos_gain: float32 [1536], replicated, may hold values from 0.25 to 1.75
- w_first: bfloat16 [1536, 3072], P(('grp', 'tile'), 'tp'), may hold values from -0.15625 to 0.15625
- w_second: bfloat16 [1536, 3072], P(('grp', 'tile'), 'tp'), may hold values from -0.109375 to 0.109375
- flux_proj: bfloat16 [1536, 256], replicated, may hold values from -0.15625 to 0.15625
- remap_index: int32 [64, 3], P(('grp', 'tile', 'tp')), may hold values from 0 to 3
- remap_weight: bfloat16 [64, 3, 128, 128], P(('grp', 'tile', 'tp')), may hold values from -0.3125 to 0.3125
- ocean_state: bfloat16 [64, 128, 256], P(('grp', 'tile'), 'tp'), may hold values from -6 to 6
- depth_levels: int32 [64, 128], P(('grp', 'tile'), 'tp'), may hold values from 0 to 16
- conv_kernel: float32 [3, 3, 256], replicated, may hold values from -2 to 2
- ocean_gain: float32 [256], replicated, may hold values from 0.25 to 1.75
- ocean_w_in: bfloat16 [256, 1024], replicated, may hold values from -0.375 to 0.375
- ocean_w_out: bfloat16 [1024, 256], replicated, may hold values from -0.1875 to 0.1875
- ocean_cotangent: bfloat16 [64, 128, 256], P(('grp', 'tile'), 'tp'), may hold values from -6 to 6
Outputs:
- atmos_out: bfloat16 [4096, 1536], P(('grp', 'tile', 'tp'))
- ocean_out: bfloat16 [64, 128, 256], P(('grp', 'tile'), 'tp')
- weight_grads: float32 [2048, 256], P(('grp', 'tile', 'tp'))
Inputs may be any that keep to these rules, and one draw needn't show every extreme that they name: `remap_index`: index the 128-token blocks among the 512 atmosphere tokens of the same grp and tile indices as the ocean tile of that block. `depth_levels`: 0 marks land.
All inputs are finite; a program needn't handle non-finite values.
Results may differ from a plain program's by a relative error of at most 0.018.
Values may be sent and summed in bfloat16 or wider, within the bound.
No kernel may reach another device: no remote copies, remote signals or barrier semaphores. Data moves between devices by JAX's collectives and lax.ppermute only.
A program may use at most 64 MiB of HBM per device.

v0:
```python
import jax
import jax.numpy as jnp
from jax import lax
from jax.sharding import PartitionSpec as P

LEV = 16
epsilon = 1e-06


def with_halo(block, sides, width):
    for axis, dim in sides:
        count = lax.axis_size(axis)
        forward = [(i, i + 1) for i in range(count - 1)]
        backward = [(target, source) for source, target in forward]
        low = lax.ppermute(
            lax.slice_in_dim(block, block.shape[dim] - width, None, axis=dim), axis, forward
        )
        high = lax.ppermute(lax.slice_in_dim(block, 0, width, axis=dim), axis, backward)
        block = jnp.concatenate([low, block, high], axis=dim)
    return block


def rms_norm(values, gain):
    wide = values.astype(jnp.float32)
    scale = lax.rsqrt(jnp.mean(wide * wide, axis=-1, keepdims=True) + epsilon)
    return (wide * scale * gain).astype(jnp.bfloat16)


def on_device(
    atmos_state,
    atmos_gain,
    w_first,
    w_second,
    flux_proj,
    remap_index,
    remap_weight,
    ocean_state,
    depth_levels,
    conv_kernel,
    ocean_gain,
    ocean_w_in,
    ocean_w_out,
    ocean_cotangent,
):
    normed = rms_norm(atmos_state, atmos_gain)
    rows_all = atmos_state.shape[0]
    hsum = jnp.dot(
        normed,
        lax.all_gather(w_first, ("grp", "tile"), axis=0, tiled=True),
        preferred_element_type=jnp.float32,
    )
    hidden = jax.nn.gelu(hsum).astype(jnp.bfloat16)
    partial_sum = lax.dot_general(
        hidden,
        lax.all_gather(w_second, ("grp", "tile"), axis=0, tiled=True),
        (((1,), (1,)), ((), ())),
        preferred_element_type=jnp.float32,
    )
    rows_own = rows_all // lax.axis_size("tp")
    block_rows = remap_weight.shape[2]
    channels = flux_proj.shape[1]
    summed = lax.psum_scatter(
        partial_sum.astype(jnp.bfloat16), "tp", scatter_dimension=0, tiled=True
    ).astype(jnp.float32)
    own_rows = lax.dynamic_slice_in_dim(atmos_state, lax.axis_index("tp") * rows_own, rows_own, 0)
    atmos_out = (own_rows.astype(jnp.float32) + summed).astype(jnp.bfloat16)
    flux = jnp.dot(atmos_out, flux_proj, preferred_element_type=jnp.float32).astype(jnp.bfloat16)
    piece = lax.all_gather(flux, "tp", axis=0, tiled=True)
    count = piece.shape[0] // block_rows
    blocks = piece.reshape(count, block_rows, channels)
    targets = jnp.arange(count, dtype=jnp.int32)
    select = (remap_index[:, :, None] == targets[None, None, :]).astype(jnp.bfloat16)
    picked = jnp.einsum("bkj,jrc->bkrc", select, blocks, preferred_element_type=jnp.float32).astype(
        jnp.bfloat16
    )
    remapped = jnp.einsum(
        "bksr,bkrc->bsc", remap_weight, picked, preferred_element_type=jnp.float32
    )
    tile_x, tile_y, _ = ocean_state.shape
    levels = jnp.arange(channels, dtype=jnp.int32) // (channels // LEV)
    wet = (levels[None, None, :] < depth_levels[:, :, None]).astype(jnp.float32)
    moved = remapped.astype(jnp.bfloat16).reshape(tile_x, tile_y, channels)
    field = ((ocean_state.astype(jnp.float32) + moved.astype(jnp.float32)) * wet).astype(
        jnp.bfloat16
    )
    padded = with_halo(field, ((("grp", "tile"), 0), ("tp", 1)), 1).astype(jnp.float32)
    conv = jnp.zeros((tile_x, tile_y, channels), jnp.float32)
    for i in range(3):
        for j in range(3):
            conv = conv + conv_kernel[i, j] * padded[i : i + tile_x, j : j + tile_y]
    centred = conv - jnp.mean(conv, axis=-1, keepdims=True)
    variance = jnp.mean(centred * centred, axis=-1, keepdims=True)
    cells = tile_x * tile_y
    ocean_normed = (
        (centred * lax.rsqrt(variance + epsilon) * ocean_gain)
        .astype(jnp.bfloat16)
        .reshape(cells, channels)
    )
    flat_field = field.reshape(cells, channels)
    flat_wet = wet.reshape(cells, channels)
    pre = jnp.dot(ocean_normed, ocean_w_in, preferred_element_type=jnp.float32)
    activated, backward = jax.vjp(jax.nn.gelu, pre)
    activated = activated.astype(jnp.bfloat16)
    out = jnp.dot(activated, ocean_w_out, preferred_element_type=jnp.float32)
    ocean_out = (
        ((flat_field.astype(jnp.float32) + out) * flat_wet)
        .astype(jnp.bfloat16)
        .reshape(tile_x, tile_y, channels)
    )
    dout = (ocean_cotangent.reshape(cells, channels).astype(jnp.float32) * flat_wet).astype(
        jnp.bfloat16
    )
    dact = lax.dot_general(
        dout, ocean_w_out, (((1,), (1,)), ((), ())), preferred_element_type=jnp.float32
    )
    dpre = backward(dact)[0].astype(jnp.bfloat16)
    grad_in = lax.dot_general(
        dpre, ocean_normed, (((0,), (0,)), ((), ())), preferred_element_type=jnp.float32
    )
    grad_out = lax.dot_general(
        activated, dout, (((0,), (0,)), ((), ())), preferred_element_type=jnp.float32
    )
    terms = jnp.concatenate([grad_in, grad_out], axis=0)
    weight_grads = lax.psum_scatter(terms, ("grp", "tile", "tp"), scatter_dimension=0, tiled=True)
    return (atmos_out, ocean_out, weight_grads)


def solution(mesh):
    in_specs = (
        P(("grp", "tile"), None),
        P(),
        P(("grp", "tile"), "tp"),
        P(("grp", "tile"), "tp"),
        P(),
        P(("grp", "tile", "tp"), None),
        P(("grp", "tile", "tp"), None, None, None),
        P(("grp", "tile"), "tp", None),
        P(("grp", "tile"), "tp"),
        P(),
        P(),
        P(),
        P(),
        P(("grp", "tile"), "tp", None),
    )
    out_specs = (
        P(("grp", "tile", "tp"), None),
        P(("grp", "tile"), "tp", None),
        P(("grp", "tile", "tp"), None),
    )
    return jax.shard_map(
        on_device, mesh=mesh, in_specs=in_specs, out_specs=out_specs, check_vma=False
    )
```

profile of v0, /device:TPU:0, one launch (start us, length us, event | category | flops | bytes accessed | tf_op | source)
XLA Modules:
  0.0 300.5 jit_solution(9202283299108384426)
XLA Ops:
  7.2 0.0 copy-start
  7.2 0.0 all-gather.5.cloned.1.call-start
  7.2 0.7 all-gather.5.cloned.1.call-update
  7.9 0.0 all-gather.3.cloned.1.call-start
  8.0 0.7 all-gather.3.cloned.1.call-update
  8.7 0.0 reduce-scatter.3.cloned.1.call-start
  8.7 1.8 fusion
  10.5 31.0 %all-gather.5.cloned.1.call-done = bf16[1536,768]{1,0:T(8,128)(2,1)} async-done(((bf16[192,768]{1,0:T(8,128)(2,1)}), bf16[1536,768]{1,0:T(8,128)(2,1)}) %all-gather.5.cloned.1.call-update) | async-done | bytes 2359312 | tf_op jit(solution)/shard_map/all_gather | solution.py:55
  41.5 30.8 %all-gather.3.cloned.1.call-done = bf16[1536,768]{1,0:T(8,128)(2,1)} async-done(((bf16[192,768]{1,0:T(8,128)(2,1)}), bf16[1536,768]{1,0:T(8,128)(2,1)}) %all-gather.3.cloned.1.call-update) | async-done | bytes 2359312 | tf_op jit(solution)/shard_map/all_gather | solution.py:49
  72.3 6.9 %convolution_convert_fusion = bf16[512,1536]{1,0:T(8,128)(2,1)} fusion(bf16[1536,768]{1,0:T(8,128)(2,1)} %all-gather.5.cloned.1.call-done, bf16[1536,768]{1,0:T(8,128)(2,1)} %all-gather.3.cloned.1.call-done, bf16[512,1536]{1,0:T(8,128)(2,1)S(1)} %copy-done.1, f32[1536]{0:T(1024)S(1)} %copy-done.12, f32[512]{0:T(512)S(1)} %add_rsqrt_fusion.1), kind=kOutput, calls=%fused_computation.5 | convolution fusion | flops 2423390208 | bytes 7872512 | tf_op jit(solution)/shard_map/dot_general | solution.py:53
  79.2 0.0 reduce-scatter.3.cloned.1.call-update
  79.2 0.0 copy-start.9
  79.2 0.0 reduce-scatter.5.cloned.1.call-start
  79.3 0.6 copy-done.7
  79.9 0.1 lt.27
  80.0 34.8 %reduce-scatter.3.cloned.1.call-done = bf16[128,1536]{1,0:T(8,128)(2,1)} async-done(((bf16[512,1536]{1,0:T(8,128)(2,1)}), bf16[128,1536]{1,0:T(8,128)(2,1)}) %reduce-scatter.3.cloned.1.call-update) | async-done | bytes 393232 | tf_op jit(solution)/shard_map/reduce_scatter | solution.py:62
  114.8 1.1 add_convert_fusion
  115.9 0.0 copy-start.2
  115.9 0.0 copy-start.6
  116.0 0.3 convolution_convert_fusion.1
  116.2 0.0 copy-start.5
  116.3 0.0 copy-start.8
  116.3 14.6 %all_gather.11 = bf16[512,256]{1,0:T(8,128)(2,1)S(1)} all-gather(bf16[128,256]{1,0:T(8,128)(2,1)S(1)} %convolution_convert_fusion.1), channel_id=1, replica_groups=mesh['grp'=2,'tile'=4,'tp'=4] {'tp'}, dimensions={0}, use_global_device_ids=true | all-gather | bytes 327680 | tf_op jit(solution)/shard_map/all_gather | solution.py:68
  130.8 0.4 fusion.41
  131.2 0.2 fusion.19
  131.5 0.1 select_convert_fusion
  131.6 1.3 collective-permute-start.1
  132.9 3.0 %collective-permute-start = (bf16[1,32,256]{2,1,0:T(8,128)(2,1)S(1)}, bf16[1,32,256]{2,1,0:T(8,128)(2,1)S(1)}, u32[]{:S(2)}, u32[]{:S(2)}) collective-permute-start(bf16[1,32,256]{2,1,0:T(8,128)(2,1)S(1)} %get-tuple-element.7), channel_id=1, source_target_pairs={{0,4},{4,8},{8,12},{12,16},{16,20},{20,24},{24,28},{1,5},{5,9},{9,... | collective-permute-start | bytes 49160 | tf_op jit(solution)/shard_map/ppermute | solution.py:15
  136.0 0.1 fusion.32
  136.1 0.7 collective-permute-done
  136.8 1.3 collective-permute-start.3
  138.1 4.5 %collective-permute-start.2 = (bf16[10,1,256]{2,1,0:T(2,128)(2,1)S(1)}, bf16[10,1,256]{2,1,0:T(2,128)(2,1)S(1)}, u32[]{:S(2)}, u32[]{:S(2)}) collective-permute-start(bf16[10,1,256]{2,1,0:T(2,128)(2,1)S(1)} %get-tuple-element.5), channel_id=1, source_target_pairs={{0,1},{1,2},{2,3},{4,5},{5,6},{6,7},{8,9},{9,10},{10,11},{12,13},{... | collective-permute-start | bytes 15368 | tf_op jit(solution)/shard_map/ppermute | solution.py:15
  142.7 1.3 collective-permute-done.2
  144.0 0.1 maximum_convert_fusion
  144.1 0.0 copy-start.3
  144.1 0.3 fusion.57
  144.4 0.2 multiply_reduce_fusion
  144.6 0.2 copy-done.10
  144.8 0.1 multiply_convert_fusion.1
  144.9 0.2 copy-done.3
  145.1 0.3 fusion.63
  145.4 0.6 fusion.56
  146.0 3.1 %fusion.30 = f32[1024,256]{1,0:T(8,128)} fusion(bf16[256,256]{1,0:T(8,128)(2,1)S(1)} %bitcast.50, f32[256,1024]{1,0:T(8,128)S(1)} %fusion.63, bf16[256,256]{1,0:T(8,128)(2,1)S(1)} %fusion.32, bf16[1024,256]{1,0:T(8,128)(2,1)} %param.26), kind=kOutput, calls=%fused_computation.38 | convolution fusion | flops 273678336 | bytes 2883584 | tf_op jit(solution)/shard_map/dot_general | solution.py:117
  149.2 2.7 pad_maximum_fusion
  151.9 0.0 reduce-scatter.5.cloned.1.call-update
  151.9 1.0 copy-done.11
  152.9 1.1 fusion.20
  154.0 139.9 %reduce-scatter.5.cloned.1.call-done = f32[64,256]{1,0:T(8,128)} async-done(((f32[2048,256]{1,0:T(8,128)}), f32[64,256]{1,0:T(8,128)}) %reduce-scatter.5.cloned.1.call-update) | async-done | bytes 65552 | tf_op jit(solution)/shard_map/reduce_scatter | solution.py:124
  (24 shorter events, 0.1 us)
Async XLA Ops:
  7.2 108.8 %copy-start = (bf16[1536,256]{1,0:T(8,128)(2,1)S(1)}, bf16[1536,256]{1,0:T(8,128)(2,1)}, u32[]{:S(2)}) copy-start(bf16[1536,256]{1,0:T(8,128)(2,1)} %param.18) | copy-start | bytes 2359300
  7.2 65.1 %copy-start.1 = (bf16[512,1536]{1,0:T(8,128)(2,1)S(1)}, bf16[512,1536]{1,0:T(8,128)(2,1)}, u32[]{:S(2)}) copy-start(bf16[512,1536]{1,0:T(8,128)(2,1)} %param.14) | copy-start | bytes 4718596
  7.2 65.1 %copy-start.12 = (f32[1536]{0:T(1024)S(1)}, f32[1536]{0:T(1024)}, u32[]{:S(2)}) copy-start(f32[1536]{0:T(1024)} %param.15) | copy-start | bytes 18436
  7.2 34.3 %all-gather.5.cloned.1.call-start = ((), (), s32[]{:S(2)}) async-start(), calls=%async_computation.3 | async-start | bytes 2654208 | tf_op jit(solution)/shard_map/all_gather | solution.py:55
  7.9 64.4 %all-gather.3.cloned.1.call-start = ((), (), s32[]{:S(2)}) async-start(), calls=%async_computation.2 | async-start | bytes 2654208 | tf_op jit(solution)/shard_map/all_gather | solution.py:49
  8.7 106.1 %reduce-scatter.3.cloned.1.call-start = ((), (), s32[]{:S(2)}) async-start(), calls=%async_computation.4 | async-start | bytes 1966080 | tf_op jit(solution)/shard_map/reduce_scatter | solution.py:62
  79.2 0.7 copy-start.7
  79.2 51.6 %copy-start.9 = (s32[2,3]{1,0:T(2,128)S(1)}, s32[2,3]{1,0:T(2,128)}, u32[]{:S(2)}) copy-start(s32[2,3]{1,0:T(2,128)} %param.19) | copy-start | bytes 76
  79.2 214.7 %reduce-scatter.5.cloned.1.call-start = ((), (), s32[]{:S(2)}) async-start(), calls=%async_computation.5 | async-start | bytes 2162688 | tf_op jit(solution)/shard_map/reduce_scatter | solution.py:124
  80.0 51.2 %copy-start.4 = (bf16[2,3,128,128]{3,2,1,0:T(8,128)(2,1)S(1)}, bf16[2,3,128,128]{3,2,1,0:T(8,128)(2,1)}, u32[]{:S(2)}) copy-start(bf16[2,3,128,128]{3,2,1,0:T(8,128)(2,1)} %param.20) | copy-start | bytes 589828
  115.9 15.5 %copy-start.2 = (bf16[128,1536]{1,0:T(8,128)(2,1)}, bf16[128,1536]{1,0:T(8,128)(2,1)S(1)}, u32[]{:S(2)}) copy-start(bf16[128,1536]{1,0:T(8,128)(2,1)S(1)} %add_convert_fusion) | copy-start | bytes 1179652
  115.9 15.5 %copy-start.6 = (bf16[8,32,256]{2,1,0:T(8,128)(2,1)S(1)}, bf16[8,32,256]{2,1,0:T(8,128)(2,1)}, u32[]{:S(2)}) copy-start(bf16[8,32,256]{2,1,0:T(8,128)(2,1)} %param.21) | copy-start | bytes 393220
  116.2 19.7 %copy-start.5 = (bf16[8,32,256]{2,1,0:T(8,128)(2,1)S(1)}, bf16[8,32,256]{2,1,0:T(8,128)(2,1)}, u32[]{:S(2)}) copy-start(bf16[8,32,256]{2,1,0:T(8,128)(2,1)} %param.27) | copy-start | bytes 393220
  116.3 26.4 %copy-start.8 = (f32[3,3,256]{2,1,0:T(4,128)S(1)}, f32[3,3,256]{2,1,0:T(4,128)}, u32[]{:S(2)}) copy-start(f32[3,3,256]{2,1,0:T(4,128)} %param.23) | copy-start | bytes 27652
  131.6 4.5 %collective-permute-start.1 = (bf16[1,32,256]{2,1,0:T(8,128)(2,1)S(1)}, bf16[1,32,256]{2,1,0:T(8,128)(2,1)S(1)}, u32[]{:S(2)}, u32[]{:S(2)}) collective-permute-start(bf16[1,32,256]{2,1,0:T(8,128)(2,1)S(1)} %get-tuple-element.8), channel_id=1, source_target_pairs={{4,0},{8,4},{12,8},{16,12},{20,16},{24,20},{28,24},{5,1},{9,5},{13... | collective-permute-start | bytes 49160 | tf_op jit(solution)/shard_map/ppermute | solution.py:18
  132.9 3.9 %collective-permute-start = (bf16[1,32,256]{2,1,0:T(8,128)(2,1)S(1)}, bf16[1,32,256]{2,1,0:T(8,128)(2,1)S(1)}, u32[]{:S(2)}, u32[]{:S(2)}) collective-permute-start(bf16[1,32,256]{2,1,0:T(8,128)(2,1)S(1)} %get-tuple-element.7), channel_id=1, source_target_pairs={{0,4},{4,8},{8,12},{12,16},{16,20},{20,24},{24,28},{1,5},{5,9},{9,... | collective-permute-start | bytes 49160 | tf_op jit(solution)/shard_map/ppermute | solution.py:15
  136.8 5.9 %collective-permute-start.3 = (bf16[10,1,256]{2,1,0:T(2,128)(2,1)S(1)}, bf16[10,1,256]{2,1,0:T(2,128)(2,1)S(1)}, u32[]{:S(2)}, u32[]{:S(2)}) collective-permute-start(bf16[10,1,256]{2,1,0:T(2,128)(2,1)S(1)} %get-tuple-element.6), channel_id=1, source_target_pairs={{1,0},{2,1},{3,2},{5,4},{6,5},{7,6},{9,8},{10,9},{11,10},{13,12},{... | collective-permute-start | bytes 15368 | tf_op jit(solution)/shard_map/ppermute | solution.py:18
  138.1 5.9 %collective-permute-start.2 = (bf16[10,1,256]{2,1,0:T(2,128)(2,1)S(1)}, bf16[10,1,256]{2,1,0:T(2,128)(2,1)S(1)}, u32[]{:S(2)}, u32[]{:S(2)}) collective-permute-start(bf16[10,1,256]{2,1,0:T(2,128)(2,1)S(1)} %get-tuple-element.5), channel_id=1, source_target_pairs={{0,1},{1,2},{2,3},{4,5},{5,6},{6,7},{8,9},{9,10},{10,11},{12,13},{... | collective-permute-start | bytes 15368 | tf_op jit(solution)/shard_map/ppermute | solution.py:15
  144.1 0.7 copy-start.10
  144.1 1.0 copy-start.3
  151.9 1.0 copy-start.11
Sparse Core Ops, SparseCore 0:
  9.9 31.5 all-gather.4
  43.4 28.8 all-gather.2
  79.3 35.4 reduce-scatter.2
  152.0 141.8 reduce-scatter.4
where the time goes:
time: 301 us; the launch traced here: 300 us
  waiting for transfers between devices  240 us (80%)
  blocking collectives  14.6 us (5%)
  between operations  14 us (5%)
  matrix products  12.9 us (4%)
  starting transfers between devices  10.3 us (3%)
  other arithmetic  6.51 us (2%)
    reduce_scatter x1, waiting for transfers between devices, on_device(): lax.psum_scatter(terms, ('grp', 'tile', 'tp'), scatter_dimension=0, tiled...  140 us
    reduce_scatter x1, waiting for transfers between devices, on_device(): lax.psum_scatter(partial_sum.astype(jnp.bfloat16), 'tp', scatter_dimensio...  34.8 us
    all_gather x1, waiting for transfers between devices, on_device(): lax.all_gather(w_second, ('grp', 'tile'), axis=0, tiled=True)  31 us
    all_gather x1, waiting for transfers between devices, on_device(): lax.all_gather(w_first, ('grp', 'tile'), axis=0, tiled=True)  30.8 us
    all_gather x1, blocking collectives, on_device(): piece = lax.all_gather(flux, 'tp', axis=0, tiled=True)  14.6 us
    ppermute x2, starting transfers between devices, with_halo(): lax.ppermute(lax.slice_in_dim(block, block.shape[dim] - width, None, axis...  7.58 us
    dot_general x1, matrix products, on_device(): lax.dot_general(hidden, lax.all_gather(w_second, ('grp', 'tile'), axis=0,...  6.86 us
  transfers between devices with their start and end apart: 8, of which 6 were waited for; matrix products, arithmetic and copies ran while one was open for 1% of the time, Pallas kernels for 0%

commit v1 on v0

--- a/solution.py
+++ b/solution.py
@@ -5,6 +5,18 @@
 
 LEV = 16
 epsilon = 1e-06
+
+
+def collect(value, axis, dim):
+    ways, here, step = (lax.axis_size(axis), lax.axis_index(axis), value.shape[dim])
+    line, have = (value, 1)
+    while have < ways:
+        line = jnp.concatenate(
+            [line, lax.ppermute(line, axis, [(d, (d - have) % ways) for d in range(ways)])],
+            axis=dim,
+        )
+        have = 2 * have
+    return jnp.roll(line, here * step, axis=dim)
 
 
 def with_halo(block, sides, width):
@@ -52,7 +64,7 @@
     hidden = jax.nn.gelu(hsum).astype(jnp.bfloat16)
     partial_sum = lax.dot_general(
         hidden,
-        lax.all_gather(w_second, ("grp", "tile"), axis=0, tiled=True),
+        collect(w_second, ("grp", "tile"), 0),
         (((1,), (1,)), ((), ())),
         preferred_element_type=jnp.float32,
     )

time: 301 us -> 305 us (1.013)
  waiting for transfers between devices: 240 us -> 230 us
  local copies, waits for them, and re-layouts: 2.17 us -> 7 us
  starting transfers between devices: 10.3 us -> 15.1 us
  other arithmetic: 6.51 us -> 9.71 us
    ppermute x0 -> x3, waiting for transfers between devices: none -> 52 us  [collect(): lax.ppermute(line, axis, [(d, (d - have) % ways) for d in range(ways)])]
    all_gather x1 -> x0, waiting for transfers between devices: 31 us -> none  [on_device(): lax.all_gather(w_second, ('grp', 'tile'), axis=0, tiled=True)]
    all_gather x1, waiting for transfers between devices: 30.8 us -> 0.01 us  [on_device(): lax.all_gather(w_first, ('grp', 'tile'), axis=0, tiled=True)]
    ppermute x0 -> x3, starting transfers between devices: none -> 4.67 us  [collect(): lax.ppermute(line, axis, [(d, (d - have) % ways) for d in range(ways)])]
    unnamed x26 -> x31, local copies, waits for them, and re-layouts: 2.08 us -> 5.81 us
    concatenate x0 -> x2, other arithmetic: none -> 3.09 us  [collect(): jnp.concatenate([line, lax.ppermute(line, axis, [(d, (d - have) % ways) f...]
  transfers between devices with their start and end apart: 8 -> 10, of which waited for: 6 -> 7; matrix products, arithmetic and copies ran while one was open for 1% -> 5% of each run, Pallas kernels for 0% -> 0%
where the time goes in v1:
time: 305 us
  waiting for transfers between devices  230 us (75%)
  starting transfers between devices  15.1 us (5%)
  matrix products  14.5 us (5%)
  blocking collectives  14.4 us (5%)
  between operations  14 us (5%)
  other arithmetic  9.71 us (3%)
  local copies, waits for them, and re-layouts  7 us (2%)
    reduce_scatter x1, waiting for transfers between devices, on_device(): lax.psum_scatter(terms, ('grp', 'tile', 'tp'), scatter_dimension=0, tiled...  140 us
    ppermute x3, waiting for transfers between devices, collect(): lax.ppermute(line, axis, [(d, (d - have) % ways) for d in range(ways)])  52 us
    reduce_scatter x1, waiting for transfers between devices, on_device(): lax.psum_scatter(partial_sum.astype(jnp.bfloat16), 'tp', scatter_dimensio...  35.7 us
    all_gather x1, blocking collectives, on_device(): piece = lax.all_gather(flux, 'tp', axis=0, tiled=True)  14.4 us
    ppermute x2, starting transfers between devices, with_halo(): lax.ppermute(lax.slice_in_dim(block, block.shape[dim] - width, None, axis...  7.58 us
    dot_general x1, matrix products, on_device(): lax.dot_general(hidden, collect(w_second, ('grp', 'tile'), 0), (((1,), (1...  7.46 us
  transfers between devices with their start and end apart: 10, of which 7 were waited for; matrix products, arithmetic and copies ran while one was open for 5% of the time, Pallas kernels for 0%

profile of v1, /device:TPU:0, one launch (start us, length us, event | category | flops | bytes accessed | tf_op | source)
XLA Modules:
  0.0 304.9 jit_solution(11417044663771471322)
XLA Ops:
  7.2 0.0 all-gather.2.cloned.1.call-start
  7.2 0.7 all-gather.2.cloned.1.call-update
  7.9 0.0 reduce-scatter.3.cloned.1.call-start
  8.0 3.4 %collective-permute-start = (bf16[192,768]{1,0:T(8,128)(2,1)}, bf16[192,768]{1,0:T(8,128)(2,1)S(1)}, u32[]{:S(2)}, u32[]{:S(2)}) collective-permute-start(bf16[192,768]{1,0:T(8,128)(2,1)} %param.17), channel_id=1, source_target_pairs={{0,28},{4,0},{8,4},{12,8},{16,12},{20,16},{24,20},{28,24},{1,29},{... | collective-permute-start | bytes 884744 | tf_op jit(solution)/shard_map/ppermute | solution.py:15
  11.4 4.6 %collective-permute-done = bf16[192,768]{1,0:T(8,128)(2,1)S(1)} collective-permute-done((bf16[192,768]{1,0:T(8,128)(2,1)}, bf16[192,768]{1,0:T(8,128)(2,1)S(1)}, u32[]{:S(2)}, u32[]{:S(2)}) %collective-permute-start) | collective-permute-done | bytes 294944 | tf_op jit(solution)/shard_map/ppermute | solution.py:15
  15.9 1.0 pad_maximum_fusion.2
  16.9 0.6 collective-permute-start.1
  17.6 18.2 %collective-permute-done.1 = bf16[384,768]{1,0:T(8,128)(2,1)S(1)} collective-permute-done((bf16[384,768]{1,0:T(8,128)(2,1)S(1)}, bf16[384,768]{1,0:T(8,128)(2,1)S(1)}, u32[]{:S(2)}, u32[]{:S(2)}) %collective-permute-start.1) | collective-permute-done | bytes 589856 | tf_op jit(solution)/shard_map/ppermute | solution.py:15
  35.8 2.1 pad_maximum_fusion.1
  37.9 0.6 collective-permute-start.2
  38.5 0.7 constant_dynamic-update-slice_fusion.7
  39.2 1.8 fusion
  41.0 0.7 constant_dynamic-update-slice_fusion.6
  41.8 0.9 constant_dynamic-update-slice_fusion.5
  42.6 29.2 %collective-permute-done.2 = bf16[768,768]{1,0:T(8,128)(2,1)S(1)} collective-permute-done((bf16[768,768]{1,0:T(8,128)(2,1)}, bf16[768,768]{1,0:T(8,128)(2,1)S(1)}, u32[]{:S(2)}, u32[]{:S(2)}) %collective-permute-start.2) | collective-permute-done | bytes 1179680 | tf_op jit(solution)/shard_map/ppermute | solution.py:15
  71.8 1.1 constant_dynamic-update-slice_fusion.4
  72.9 0.7 constant_dynamic-update-slice_fusion.3
  73.7 0.7 constant_dynamic-update-slice_fusion.2
  74.4 0.9 constant_dynamic-update-slice_fusion.1
  75.3 1.1 constant_dynamic-update-slice_fusion
  76.4 7.5 %convolution_convert_fusion = bf16[512,1536]{1,0:T(8,128)(2,1)} fusion(bf16[3072,768]{1,0:T(8,128)(2,1)} %constant_dynamic-update-slice_fusion, s32[]{:T(128)S(6)} %select_n.29, bf16[1536,768]{1,0:T(8,128)(2,1)} %all-gather.2.cloned.1.call-done, bf16[512,1536]{1,0:T(8,128)(2,1)} %param.14, f32[1536]{0:T(1024)S(1)} %copy-done.11, f32[512]{0:T(512)S(1)} %add_rsqrt_fusion.1), kind=kOutput, calls=%fused_computation.5 | convolution fusion | flops 2423390208 | bytes 7872516 | tf_op jit(solution)/shard_map/dot_general | solution.py:65
  83.8 0.0 reduce-scatter.3.cloned.1.call-update
  83.9 0.0 reduce-scatter.5.cloned.1.call-start
  83.9 0.1 lt.41
  84.0 35.7 %reduce-scatter.3.cloned.1.call-done = bf16[128,1536]{1,0:T(8,128)(2,1)} async-done(((bf16[512,1536]{1,0:T(8,128)(2,1)}), bf16[128,1536]{1,0:T(8,128)(2,1)}) %reduce-scatter.3.cloned.1.call-update) | async-done | bytes 393232 | tf_op jit(solution)/shard_map/reduce_scatter | solution.py:74
  119.7 1.2 add_convert_fusion
  120.9 0.3 convolution_convert_fusion.1
  121.2 14.4 %all_gather.7 = bf16[512,256]{1,0:T(8,128)(2,1)S(1)} all-gather(bf16[128,256]{1,0:T(8,128)(2,1)S(1)} %convolution_convert_fusion.1), channel_id=1, replica_groups=mesh['grp'=2,'tile'=4,'tp'=4] {'tp'}, dimensions={0}, use_global_device_ids=true | all-gather | bytes 327680 | tf_op jit(solution)/shard_map/all_gather | solution.py:80
  135.7 0.4 fusion.42
  136.0 0.2 fusion.20
  136.3 0.1 select_convert_fusion
  136.4 1.4 collective-permute-start.4
  137.9 3.0 collective-permute-start.3
  140.9 0.1 fusion.33
  141.0 0.7 collective-permute-done.3
  141.7 1.3 collective-permute-start.6
  143.0 4.5 %collective-permute-start.5 = (bf16[10,1,256]{2,1,0:T(2,128)(2,1)S(1)}, bf16[10,1,256]{2,1,0:T(2,128)(2,1)S(1)}, u32[]{:S(2)}, u32[]{:S(2)}) collective-permute-start(bf16[10,1,256]{2,1,0:T(2,128)(2,1)S(1)} %get-tuple-element.5), channel_id=1, source_target_pairs={{0,1},{1,2},{2,3},{4,5},{5,6},{6,7},{8,9},{9,10},{10,11},{12,13},{... | collective-permute-start | bytes 15368 | tf_op jit(solution)/shard_map/ppermute | solution.py:27
  147.6 1.3 collective-permute-done.5
  149.0 0.1 maximum_convert_fusion
  149.0 0.3 fusion.59
  149.3 0.2 multiply_reduce_fusion
  149.5 0.1 multiply_convert_fusion.1
  149.7 0.3 fusion.65
  150.0 0.6 fusion.58
  150.6 3.1 %fusion.31 = f32[1024,256]{1,0:T(8,128)} fusion(bf16[256,256]{1,0:T(8,128)(2,1)S(1)} %bitcast.49, f32[256,1024]{1,0:T(8,128)S(1)} %fusion.65, bf16[256,256]{1,0:T(8,128)(2,1)S(1)} %fusion.33, bf16[1024,256]{1,0:T(8,128)(2,1)} %param.26), kind=kOutput, calls=%fused_computation.41 | convolution fusion | flops 273678336 | bytes 2883584 | tf_op jit(solution)/shard_map/dot_general | solution.py:129
  153.7 2.7 pad_maximum_fusion
  156.4 2.2 fusion.21
  158.6 139.8 %reduce-scatter.5.cloned.1.call-done = f32[64,256]{1,0:T(8,128)} async-done(((f32[2048,256]{1,0:T(8,128)}), f32[64,256]{1,0:T(8,128)}) %reduce-scatter.5.cloned.1.call-update) | async-done | bytes 65552 | tf_op jit(solution)/shard_map/reduce_scatter | solution.py:136
  (35 shorter events, 0.1 us)
Async XLA Ops:
  7.2 113.7 %copy-start = (bf16[1536,256]{1,0:T(8,128)(2,1)S(1)}, bf16[1536,256]{1,0:T(8,128)(2,1)}, u32[]{:S(2)}) copy-start(bf16[1536,256]{1,0:T(8,128)(2,1)} %param.18) | copy-start | bytes 2359300
  7.2 31.3 %copy-start.1 = (bf16[192,768]{1,0:T(8,128)(2,1)S(1)}, bf16[192,768]{1,0:T(8,128)(2,1)}, u32[]{:S(2)}) copy-start(bf16[192,768]{1,0:T(8,128)(2,1)} %param.17) | copy-start | bytes 884740
  7.2 69.2 %all-gather.2.cloned.1.call-start = ((), (), s32[]{:S(2)}) async-start(), calls=%async_computation.2 | async-start | bytes 2654208 | tf_op jit(solution)/shard_map/all_gather | solution.py:61
  7.9 111.8 %reduce-scatter.3.cloned.1.call-start = ((), (), s32[]{:S(2)}) async-start(), calls=%async_computation.3 | async-start | bytes 1966080 | tf_op jit(solution)/shard_map/reduce_scatter | solution.py:74
  8.0 8.0 %collective-permute-start = (bf16[192,768]{1,0:T(8,128)(2,1)}, bf16[192,768]{1,0:T(8,128)(2,1)S(1)}, u32[]{:S(2)}, u32[]{:S(2)}) collective-permute-start(bf16[192,768]{1,0:T(8,128)(2,1)} %param.17), channel_id=1, source_target_pairs={{0,28},{4,0},{8,4},{12,8},{16,12},{20,16},{24,20},{28,24},{1,29},{... | collective-permute-start | bytes 884744 | tf_op jit(solution)/shard_map/ppermute | solution.py:15
  16.9 18.8 %collective-permute-start.1 = (bf16[384,768]{1,0:T(8,128)(2,1)S(1)}, bf16[384,768]{1,0:T(8,128)(2,1)S(1)}, u32[]{:S(2)}, u32[]{:S(2)}) collective-permute-start(bf16[384,768]{1,0:T(8,128)(2,1)S(1)} %pad_maximum_fusion.2), channel_id=1, source_target_pairs={{0,24},{4,28},{8,0},{12,4},{16,8},{20,12},{24,16},{28,20},{1,25},{... | collective-permute-start | bytes 1769480 | tf_op jit(solution)/shard_map/ppermute | solution.py:15
  37.9 33.9 %collective-permute-start.2 = (bf16[768,768]{1,0:T(8,128)(2,1)}, bf16[768,768]{1,0:T(8,128)(2,1)S(1)}, u32[]{:S(2)}, u32[]{:S(2)}) collective-permute-start(bf16[768,768]{1,0:T(8,128)(2,1)} %pad_maximum_fusion.1), channel_id=1, source_target_pairs={{0,16},{4,20},{8,24},{12,28},{16,0},{20,4},{24,8},{28,12},{1,17},{... | collective-permute-start | bytes 3538952 | tf_op jit(solution)/shard_map/ppermute | solution.py:15
  72.9 3.4 %copy-start.11 = (f32[1536]{0:T(1024)S(1)}, f32[1536]{0:T(1024)}, u32[]{:S(2)}) copy-start(f32[1536]{0:T(1024)} %param.15) | copy-start | bytes 18436
  76.4 7.6 %copy-start.7 = (s32[8,32]{1,0:T(8,128)S(1)}, s32[8,32]{1,0:T(8,128)}, u32[]{:S(2)}) copy-start(s32[8,32]{1,0:T(8,128)} %param.22) | copy-start | bytes 3076
  83.8 51.8 %copy-start.9 = (s32[2,3]{1,0:T(2,128)S(1)}, s32[2,3]{1,0:T(2,128)}, u32[]{:S(2)}) copy-start(s32[2,3]{1,0:T(2,128)} %param.19) | copy-start | bytes 76
  83.8 52.2 %copy-start.4 = (bf16[2,3,128,128]{3,2,1,0:T(8,128)(2,1)S(1)}, bf16[2,3,128,128]{3,2,1,0:T(8,128)(2,1)}, u32[]{:S(2)}) copy-start(bf16[2,3,128,128]{3,2,1,0:T(8,128)(2,1)} %param.20) | copy-start | bytes 589828
  83.9 52.4 %copy-start.6 = (bf16[8,32,256]{2,1,0:T(8,128)(2,1)S(1)}, bf16[8,32,256]{2,1,0:T(8,128)(2,1)}, u32[]{:S(2)}) copy-start(bf16[8,32,256]{2,1,0:T(8,128)(2,1)} %param.21) | copy-start | bytes 393220
  83.9 214.5 %reduce-scatter.5.cloned.1.call-start = ((), (), s32[]{:S(2)}) async-start(), calls=%async_computation.4 | async-start | bytes 2162688 | tf_op jit(solution)/shard_map/reduce_scatter | solution.py:136
  84.0 56.9 %copy-start.5 = (bf16[8,32,256]{2,1,0:T(8,128)(2,1)S(1)}, bf16[8,32,256]{2,1,0:T(8,128)(2,1)}, u32[]{:S(2)}) copy-start(bf16[8,32,256]{2,1,0:T(8,128)(2,1)} %param.27) | copy-start | bytes 393220
  120.9 28.1 %copy-start.2 = (bf16[128,1536]{1,0:T(8,128)(2,1)}, bf16[128,1536]{1,0:T(8,128)(2,1)S(1)}, u32[]{:S(2)}) copy-start(bf16[128,1536]{1,0:T(8,128)(2,1)S(1)} %add_convert_fusion) | copy-start | bytes 1179652
  120.9 26.7 %copy-start.8 = (f32[3,3,256]{2,1,0:T(4,128)S(1)}, f32[3,3,256]{2,1,0:T(4,128)}, u32[]{:S(2)}) copy-start(f32[3,3,256]{2,1,0:T(4,128)} %param.23) | copy-start | bytes 27652
  136.3 13.3 %copy-start.10 = (f32[256]{0:T(256)S(1)}, f32[256]{0:T(256)}, u32[]{:S(2)}) copy-start(f32[256]{0:T(256)} %param.24) | copy-start | bytes 3076
  136.4 13.3 %copy-start.3 = (bf16[256,1024]{1,0:T(8,128)(2,1)S(1)}, bf16[256,1024]{1,0:T(8,128)(2,1)}, u32[]{:S(2)}) copy-start(bf16[256,1024]{1,0:T(8,128)(2,1)} %param.25) | copy-start | bytes 1572868
  136.4 4.6 %collective-permute-start.4 = (bf16[1,32,256]{2,1,0:T(8,128)(2,1)S(1)}, bf16[1,32,256]{2,1,0:T(8,128)(2,1)S(1)}, u32[]{:S(2)}, u32[]{:S(2)}) collective-permute-start(bf16[1,32,256]{2,1,0:T(8,128)(2,1)S(1)} %get-tuple-element.8), channel_id=1, source_target_pairs={{4,0},{8,4},{12,8},{16,12},{20,16},{24,20},{28,24},{5,1},{9,5},{13... | collective-permute-start | bytes 49160 | tf_op jit(solution)/shard_map/ppermute | solution.py:30
  137.9 3.9 %collective-permute-start.3 = (bf16[1,32,256]{2,1,0:T(8,128)(2,1)S(1)}, bf16[1,32,256]{2,1,0:T(8,128)(2,1)S(1)}, u32[]{:S(2)}, u32[]{:S(2)}) collective-permute-start(bf16[1,32,256]{2,1,0:T(8,128)(2,1)S(1)} %get-tuple-element.7), channel_id=1, source_target_pairs={{0,4},{4,8},{8,12},{12,16},{16,20},{20,24},{24,28},{1,5},{5,9},{9,... | collective-permute-start | bytes 49160 | tf_op jit(solution)/shard_map/ppermute | solution.py:27
  141.7 5.9 %collective-permute-start.6 = (bf16[10,1,256]{2,1,0:T(2,128)(2,1)S(1)}, bf16[10,1,256]{2,1,0:T(2,128)(2,1)S(1)}, u32[]{:S(2)}, u32[]{:S(2)}) collective-permute-start(bf16[10,1,256]{2,1,0:T(2,128)(2,1)S(1)} %get-tuple-element.6), channel_id=1, source_target_pairs={{1,0},{2,1},{3,2},{5,4},{6,5},{7,6},{9,8},{10,9},{11,10},{13,12},{... | collective-permute-start | bytes 15368 | tf_op jit(solution)/shard_map/ppermute | solution.py:30
  143.0 5.9 %collective-permute-start.5 = (bf16[10,1,256]{2,1,0:T(2,128)(2,1)S(1)}, bf16[10,1,256]{2,1,0:T(2,128)(2,1)S(1)}, u32[]{:S(2)}, u32[]{:S(2)}) collective-permute-start(bf16[10,1,256]{2,1,0:T(2,128)(2,1)S(1)} %get-tuple-element.5), channel_id=1, source_target_pairs={{0,1},{1,2},{2,3},{4,5},{5,6},{6,7},{8,9},{9,10},{10,11},{12,13},{... | collective-permute-start | bytes 15368 | tf_op jit(solution)/shard_map/ppermute | solution.py:27
Sparse Core Ops, SparseCore 0:
  9.9 48.6 all-gather.1
  84.0 35.6 reduce-scatter.2
  156.6 141.7 reduce-scatter.4
